TPU v7x, 128 devices: a whole 4x4x4 slice. The times are simulated.
128 devices in a mesh: rows: 2 (over core), cols: 64 (over z, y, x).
Axes of the slice: x: 4, y: 4, z: 4, core: 2. Of those that a mesh axis runs over, the one named last changes fastest.
Arguments:
- jacobian: float32 [32768, 16384], P('rows', 'cols'), may hold values from -0.046875 to 0.046875
- targets: float32 [64, 32768], P(None, 'rows'), may hold values from 0 to 1
- anchor: float32 [64, 16384], P(None, 'cols'), may hold values from -6 to 6
- precision: float32 [16384], P('cols'), may hold values from 0.3 to 3
Outputs:
- samples: float32 [64, 16384], P(None, 'cols')
All inputs are finite; a program needn't handle non-finite values.
Results may differ from a plain program's by a relative error of at most 0.0001.
Values sent between devices are 32-bit elements; how exact they have to be, the bound alone decides.
No kernel may reach another device: no remote copies, remote signals or barrier semaphores. Data moves between devices by JAX's collectives and lax.ppermute only.
A program may use at most 128 MiB of HBM per device.

v0:
```python
import math

import jax
import jax.numpy as jnp
from jax import lax
from jax.sharding import PartitionSpec as P

STEPS = 3


def sent_to_all(x, axis):
    copies = jnp.broadcast_to(x, (lax.axis_size(axis), *x.shape))
    return lax.all_to_all(copies, axis, split_axis=0, concat_axis=0, tiled=True)


def over_copies(x, axis):
    everything = sent_to_all(x, axis)
    return jnp.sum(everything, axis=0)


def body(jacobian, targets, anchor, precision):
    row_dev, col_dev = jacobian.shape
    total_params = col_dev * lax.axis_size("cols")
    clip_level = 0.2 * math.sqrt(row_dev * lax.axis_size("rows") / total_params)
    theta = anchor
    velocity = jnp.zeros_like(anchor)
    for step in range(STEPS):
        part_logits = lax.dot_general(
            theta,
            jacobian,
            (((1,), (1,)), ((), ())),
            precision=lax.Precision.HIGHEST,
            preferred_element_type=jnp.float32,
        )
        logits = lax.psum(part_logits, "cols")
        residual = jax.nn.sigmoid(logits) - targets
        gradient = over_copies(
            jnp.dot(
                residual,
                jacobian,
                precision=lax.Precision.HIGHEST,
                preferred_element_type=jnp.float32,
            ),
            "rows",
        )
        gradient = gradient + precision[None, :] * (theta - anchor)
        squares = over_copies(jnp.sum(gradient * gradient, axis=1), "cols")
        scale = jnp.minimum(1.0, clip_level / jnp.sqrt(squares / total_params + 1e-06))
        velocity = 0.9 * velocity + scale[:, None] * gradient
        theta = theta - 0.5 * velocity
    return theta


def solution(mesh):
    in_specs = (P("rows", "cols"), P(None, "rows"), P(None, "cols"), P("cols"))
    out_specs = P(None, "cols")
    return jax.shard_map(body, mesh=mesh, in_specs=in_specs, out_specs=out_specs, check_vma=False)
```

profile of v0, /device:TPU:0, one launch (start us, length us, event | category | flops | bytes accessed | tf_op | source)
XLA Modules:
  0.0 590.7 jit_solution(1739237668629054743)
XLA Ops:
  6.5 0.0 all-reduce.4.cloned.1.call-start
  6.5 20.6 %fusion.28 = f32[64,16384]{1,0:T(8,128)} fusion(f32[64,256]{1,0:T(8,128)} %param.6, f32[16384,256]{1,0:T(8,128)} %param.4), kind=kOutput, calls=%fused_computation.41 | convolution fusion | flops 3221225472 | bytes 21037056 | tf_op jit(solution)/shard_map/dot_general | solution.py:28
  27.2 0.0 all-reduce.4.cloned.1.call-update
  27.2 0.0 copy-start
  27.2 0.0 copy-start.1
  27.2 0.0 all-reduce.6.cloned.1.call-start
  27.3 141.7 %all-reduce.4.cloned.1.call-done = f32[64,16384]{1,0:T(8,128)} async-done(((f32[64,16384]{1,0:T(8,128)}), f32[64,16384]{1,0:T(8,128)}) %all-reduce.4.cloned.1.call-update) | async-done | bytes 4194320 | tf_op jit(solution)/shard_map/psum | solution.py:35
  168.9 14.2 %fusion.12 = f32[64,256]{1,0:T(8,128)S(1)} fusion(f32[16384,256]{1,0:T(8,128)} %param.4, f32[64,16384]{1,0:T(8,128)} %param.5, f32[64,16384]{1,0:T(8,128)} %all-reduce.4.cloned.1.call-done), kind=kOutput, calls=%fused_computation.12 | convolution fusion | flops 3225419776 | bytes 25231360 | tf_op jit(solution)/shard_map/dot_general | solution.py:38
  183.1 3.8 all_to_all.33
  187.0 0.0 copy-done
  187.0 0.0 copy-done.1
  187.0 0.1 multiply_reduce_fusion.2
  187.1 15.9 %all_to_all.34 = f32[64,1,64]{2,1,0:T(1,128)S(1)} all-to-all(f32[64,1,64]{2,1,0:T(1,128)S(1)} %broadcast_in_dim.25), channel_id=1, replica_groups=mesh['rows'=2,'cols'=64] {'cols'}, dimensions={0} | all-to-all | bytes 32768 | tf_op jit(solution)/shard_map/all_to_all | solution.py:13
  203.1 20.7 %fusion.24 = f32[64,16384]{1,0:T(8,128)} fusion(f32[16384,256]{1,0:T(8,128)} %param.4, f32[64,256]{1,0:T(8,128)S(1)} %copy-done, f32[64]{0:T(128)S(1)} %multiply_minimum_fusion.2, f32[64,256]{1,0:T(8,128)S(1)} %reduce_sum.81, f32[256]{0:T(256)S(1)} %copy-done.1), kind=kOutput, calls=%fused_computation.37 | convolution fusion | flops 3221323776 | bytes 21103872 | tf_op jit(solution)/shard_map/dot_general | solution.py:28
  223.8 0.0 all-reduce.6.cloned.1.call-update
  223.8 0.0 all-reduce.8.cloned.1.call-start
  223.9 135.1 %all-reduce.6.cloned.1.call-done = f32[64,16384]{1,0:T(8,128)} async-done(((f32[64,16384]{1,0:T(8,128)}), f32[64,16384]{1,0:T(8,128)}) %all-reduce.6.cloned.1.call-update) | async-done | bytes 4194320 | tf_op jit(solution)/shard_map/psum | solution.py:35
  359.0 14.2 %fusion.6 = f32[64,256]{1,0:T(8,128)S(1)} fusion(f32[16384,256]{1,0:T(8,128)} %param.4, f32[64,16384]{1,0:T(8,128)} %param.5, f32[64,16384]{1,0:T(8,128)} %all-reduce.6.cloned.1.call-done), kind=kOutput, calls=%fused_computation.6 | convolution fusion | flops 3225419776 | bytes 25231360 | tf_op jit(solution)/shard_map/dot_general | solution.py:38
  373.2 3.8 all_to_all.35
  377.0 0.2 multiply_reduce_fusion.1
  377.3 15.9 %all_to_all.36 = f32[64,1,64]{2,1,0:T(1,128)S(1)} all-to-all(f32[64,1,64]{2,1,0:T(1,128)S(1)} %broadcast_in_dim.27), channel_id=1, replica_groups=mesh['rows'=2,'cols'=64] {'cols'}, dimensions={0} | all-to-all | bytes 32768 | tf_op jit(solution)/shard_map/all_to_all | solution.py:13
  393.2 20.7 %fusion.21 = f32[64,16384]{1,0:T(8,128)} fusion(f32[16384,256]{1,0:T(8,128)} %param.4, f32[64]{0:T(128)S(1)} %multiply_minimum_fusion.1, f32[64]{0:T(128)S(1)} %multiply_minimum_fusion.2, f32[64,256]{1,0:T(8,128)S(1)} %reduce_sum.84, f32[64,256]{1,0:T(8,128)S(1)} %copy-done, f32[256]{0:T(256)S(1)} %copy-done.1, f32[64,256]{1,0:T(8,128)S(1)} %reduce_sum.81), kind=kOutput, calls=%fused_computation.31 | convolution fusion | flops 3221454848 | bytes 21169664 | tf_op jit(solution)/shard_map/dot_general | solution.py:28
  414.0 0.0 all-reduce.8.cloned.1.call-update
  414.0 135.2 %all-reduce.8.cloned.1.call-done = f32[64,16384]{1,0:T(8,128)} async-done(((f32[64,16384]{1,0:T(8,128)}), f32[64,16384]{1,0:T(8,128)}) %all-reduce.8.cloned.1.call-update) | async-done | bytes 4194320 | tf_op jit(solution)/shard_map/psum | solution.py:35
  549.2 14.2 %fusion = f32[64,256]{1,0:T(8,128)S(1)} fusion(f32[16384,256]{1,0:T(8,128)} %param.4, f32[64,16384]{1,0:T(8,128)} %param.5, f32[64,16384]{1,0:T(8,128)} %all-reduce.8.cloned.1.call-done), kind=kOutput, calls=%fused_computation | convolution fusion | flops 3225419776 | bytes 25231360 | tf_op jit(solution)/shard_map/dot_general | solution.py:38
  563.4 3.8 all_to_all.37
  567.2 0.2 multiply_reduce_fusion
  567.5 15.9 %all_to_all.38 = f32[64,1,64]{2,1,0:T(1,128)S(1)} all-to-all(f32[64,1,64]{2,1,0:T(1,128)S(1)} %broadcast_in_dim.29), channel_id=1, replica_groups=mesh['rows'=2,'cols'=64] {'cols'}, dimensions={0} | all-to-all | bytes 32768 | tf_op jit(solution)/shard_map/all_to_all | solution.py:13
  583.4 0.7 multiply_subtract_fusion
  (15 shorter events, 0.2 us)
Async XLA Ops:
  6.5 162.4 %all-reduce.4.cloned.1.call-start = ((), (), s32[]{:S(2)}) async-start(), calls=%async_computation.6 | async-start | bytes 8388608 | tf_op jit(solution)/shard_map/psum | solution.py:35
  27.2 159.8 %copy-start = (f32[64,256]{1,0:T(8,128)S(1)}, f32[64,256]{1,0:T(8,128)}, u32[]{:S(2)}) copy-start(f32[64,256]{1,0:T(8,128)} %param.6) | copy-start | bytes 196612
  27.2 159.8 %copy-start.1 = (f32[256]{0:T(256)S(1)}, f32[256]{0:T(256)}, u32[]{:S(2)}) copy-start(f32[256]{0:T(256)} %param.7) | copy-start | bytes 3076
  27.2 331.8 %all-reduce.6.cloned.1.call-start = ((), (), s32[]{:S(2)}) async-start(), calls=%async_computation.7 | async-start | bytes 8388608 | tf_op jit(solution)/shard_map/psum | solution.py:35
  223.8 325.4 %all-reduce.8.cloned.1.call-start = ((), (), s32[]{:S(2)}) async-start(), calls=%async_computation.8 | async-start | bytes 8388608 | tf_op jit(solution)/shard_map/psum | solution.py:35
Sparse Core Ops, SparseCore 0:
  27.3 141.5 all-reduce.3
  224.0 134.9 all-reduce.5
  414.1 135.0 all-reduce.7
where the time goes:
time: 591 us
  waiting for transfers between devices  412 us (70%)
  matrix products  105 us (18%)
  blocking collectives  59.3 us (10%)
  between operations  13.2 us (2%)
    psum x3, waiting for transfers between devices, body(): logits = lax.psum(part_logits, 'cols')  412 us
    dot_general x3, matrix products, body(): lax.dot_general(theta, jacobian, (((1,), (1,)), ((), ())), precision=lax....  62.1 us
    all_to_all x6, blocking collectives, sent_to_all(): return lax.all_to_all(copies, axis, split_axis=0, concat_axis=0, tiled=True)  59.3 us
    dot_general x3, matrix products, body(): jnp.dot(residual, jacobian, precision=lax.Precision.HIGHEST, preferred_el...  42.5 us
  transfers between devices with their start and end apart: 3, of which 3 were waited for; matrix products, arithmetic and copies ran while one was open for 0% of the time, Pallas kernels for 0%

commit v1 on v0

v1 whole, which is shorter than its diff:
```python
import math

import jax
import jax.numpy as jnp
from jax import lax
from jax.sharding import Mesh
from jax.sharding import PartitionSpec as P

STEPS = 3
SIDE = 4
CUBE = 8
SHIFT = (0, 1, 1)
AXES = ("rows", "z", "y", "x")
COLS = ("z", "y", "x")


def place(core, at):
    turned = [(p + core + s) % SIDE for p, s in zip(at, SHIFT)]
    half = [(t + 1) // 2 % 2 for t in turned]
    pair = [t // 2 for t in turned]
    return half[0] * 4 + half[1] * 2 + half[2], pair[0] * 4 + pair[1] * 2 + pair[2]


def cube_groups():
    first, second = {}, {}
    for device in range(2 * SIDE**3):
        core, z, y, x = device // 64, device // 16 % 4, device // 4 % 4, device % 4
        half, pair = place(core, (z, y, x))
        first.setdefault((core, pair), {})[half] = device
        second.setdefault((core, half), {})[pair] = device
    in_order = lambda groups: [[group[k] for k in range(CUBE)] for _, group in sorted(groups.items())]
    return in_order(first), in_order(second)


FIRST, SECOND = cube_groups()


def exchange(x, groups):
    return lax.all_to_all(x, AXES, split_axis=0, concat_axis=0, axis_index_groups=groups, tiled=True)


def copies(x, n):
    return jnp.broadcast_to(x[None], (n, *x.shape))


def own_block():
    return place(lax.axis_index("rows"), [lax.axis_index(a) for a in COLS])


def product(theta, jacobian):
    return lax.dot_general(
        theta,
        jacobian,
        (((1,), (1,)), ((), ())),
        precision=lax.Precision.HIGHEST,
        preferred_element_type=jnp.float32,
    )


def body(jacobian, targets, anchor, precision):
    samples, col_dev = anchor.shape
    row_dev = jacobian.shape[0]
    part = row_dev // CUBE
    block = part // CUBE
    total_params = col_dev * SIDE**3
    clip_level = 0.2 * math.sqrt(row_dev * 2 / total_params)
    half, pair = own_block()
    own_targets = lax.dynamic_slice(targets, (0, half * part + pair * block), (samples, block))

    def summed(x, square):
        parts = jnp.swapaxes(x.reshape(samples, CUBE, part), 0, 1)
        tail = jnp.broadcast_to(square[None, :, None], (CUBE, samples, 128))
        got = jnp.sum(exchange(jnp.concatenate([parts, tail], 2), FIRST), axis=0)
        blocks = jnp.swapaxes(got[:, :part].reshape(samples, CUBE, block), 0, 1)
        tail = jnp.broadcast_to(got[None, :, part:], (CUBE, samples, 128))
        got = jnp.sum(exchange(jnp.concatenate([blocks, tail], 2), SECOND), axis=0)
        return got[:, :block], got[:, block]

    def spread(x):
        got = exchange(copies(x, CUBE), SECOND)
        got = exchange(copies(got, CUBE), FIRST)
        return jnp.swapaxes(got.reshape(CUBE * CUBE, samples, block), 0, 1).reshape(samples, row_dev)

    def scale_of(squares):
        return jnp.minimum(1.0, clip_level / jnp.sqrt(squares / total_params + 1e-06))[:, None]

    theta = anchor
    velocity = jnp.zeros_like(anchor)
    logits, _ = summed(product(anchor, jacobian), jnp.zeros((samples,), jnp.float32))
    slope = jnp.zeros_like(logits)
    for step in range(STEPS):
        residual = spread(jax.nn.sigmoid(logits) - own_targets)
        gradient = jnp.dot(
            residual, jacobian, precision=lax.Precision.HIGHEST, preferred_element_type=jnp.float32
        )
        gradient = gradient + lax.ppermute(gradient, "rows", [(0, 1), (1, 0)])
        gradient = gradient + precision[None, :] * (theta - anchor)
        square = jnp.sum(gradient * gradient, axis=1)
        if step + 1 < STEPS:
            moved, squares = summed(product(gradient, jacobian), square)
            scale = scale_of(squares)
            slope = 0.9 * slope + scale * moved
            logits = logits - 0.5 * slope
        else:
            everything = lax.all_to_all(copies(square, SIDE**3), COLS, split_axis=0, concat_axis=0, tiled=True)
            scale = scale_of(jnp.sum(everything, axis=0))
        velocity = 0.9 * velocity + scale * gradient
        theta = theta - 0.5 * velocity
    return theta


def solution(mesh):
    cubes = Mesh(mesh.devices.reshape(2, SIDE, SIDE, SIDE), AXES)
    in_specs = (P("rows", COLS), P(None, "rows"), P(None, COLS), P(COLS))
    out_specs = P(None, COLS)
    return jax.shard_map(body, mesh=cubes, in_specs=in_specs, out_specs=out_specs, check_vma=False)
```

time: 591 us -> 419 us (0.71)
  waiting for transfers between devices: 412 us -> 14.7 us
  blocking collectives: 59.3 us -> 285 us
  matrix products: 105 us -> 78.5 us
  local copies, waits for them, and re-layouts: 0.12 us -> 14.6 us
  between operations: 13.2 us -> 0.92 us
  other arithmetic: 1.39 us -> 12.7 us
  starting transfers between devices: 0.09 us -> 6.17 us
    psum x3 -> x0, waiting for transfers between devices: 412 us -> none  [body(): logits = lax.psum(part_logits, 'cols')]
    all_to_all x6 -> x12, blocking collectives: 59.3 us -> 285 us  [the longest x11 269 us: exchange(): lax.all_to_all(x, AXES, split_axis=0, concat_axis=0, axis_index_groups=gr...]
    dot_general x3, matrix products: 42.5 us -> 28.3 us  [body(): jnp.dot(residual, jacobian, precision=lax.Precision.HIGHEST, preferred_el...]
    dot_general x3, matrix products: 62.1 us -> 50.2 us  [product(): lax.dot_general(theta, jacobian, (((1,), (1,)), ((), ())), precision=lax....]
    all_to_all x0 -> x1, waiting for transfers between devices: none -> 11 us  [exchange(): lax.all_to_all(x, AXES, split_axis=0, concat_axis=0, axis_index_groups=gr...]
    reduce_sum x9 -> x10, other arithmetic: 0.61 us -> 8.25 us  [the longest x3 7.61 us: summed(): got = jnp.sum(exchange(jnp.concatenate([parts, tail], 2), FIRST), axis=0)]
  transfers between devices with their start and end apart: 3 -> 4, of which waited for: 3 -> 4; matrix products, arithmetic and copies ran while one was open for 0% -> 0% of each run, Pallas kernels for 0% -> 0%
where the time goes in v1:
time: 419 us; the launch traced here: 413 us
  blocking collectives  285 us (68%)
  matrix products  78.5 us (19%)
  waiting for transfers between devices  14.7 us (4%)
  local copies, waits for them, and re-layouts  14.6 us (3%)
  other arithmetic  12.7 us (3%)
  starting transfers between devices  6.17 us (1%)
    all_to_all x11, blocking collectives, exchange(): lax.all_to_all(x, AXES, split_axis=0, concat_axis=0, axis_index_groups=gr...  269 us
    dot_general x3, matrix products, product(): lax.dot_general(theta, jacobian, (((1,), (1,)), ((), ())), precision=lax....  50.2 us
    dot_general x3, matrix products, body(): jnp.dot(residual, jacobian, precision=lax.Precision.HIGHEST, preferred_el...  28.3 us
    all_to_all x1, blocking collectives, body(): lax.all_to_all(copies(square, SIDE ** 3), COLS, split_axis=0, concat_axis...  16.5 us
    all_to_all x1, waiting for transfers between devices, exchange(): lax.all_to_all(x, AXES, split_axis=0, concat_axis=0, axis_index_groups=gr...  11 us
  transfers between devices with their start and end apart: 4, of which 4 were waited for; matrix products, arithmetic and copies ran while one was open for 0% of the time, Pallas kernels for 0%

profile of v1, /device:TPU:0, one launch (start us, length us, event | category | flops | bytes accessed | tf_op | source)
XLA Modules:
  0.0 412.9 jit_solution(1002321655695222412)
XLA Ops:
  0.0 18.0 %fusion.8 = f32[64,16384]{1,0:T(8,128)S(1)} fusion(f32[64,256]{1,0:T(8,128)} %param.6, f32[16384,256]{1,0:T(8,128)} %param.4), kind=kOutput, calls=%fused_computation.34 | convolution fusion | flops 3221225472 | bytes 21037056 | tf_op jit(solution)/shard_map/dot_general | solution.py:51
  18.3 0.4 concatenate.18
  18.6 35.7 %all_to_all.66 = f32[8,64,2176]{2,1,0:T(8,128)} all-to-all(f32[8,64,2176]{2,1,0:T(8,128)S(1)} %concatenate.18), channel_id=1, replica_groups={{15,12,3,0,31,28,19,16},{14,13,2,1,30,29,18,17},{11,8,7,4,27,24,23,20},..., dimensions={0} | all-to-all | bytes 8912896 | tf_op jit(solution)/shard_map/all_to_all | solution.py:39
  54.3 2.5 reduce_sum.90
  57.1 1.0 copy.90
  58.2 5.3 %all-to-all-start.1 = ((f32[8,64,384]{2,1,0:T(8,128)}), f32[8,64,384]{2,1,0:T(8,128)S(1)}, u32[]{:S(2)}, u32[]{:S(2)}) async-start(f32[8,64,384]{2,1,0:T(8,128)} %copy.90), calls=%async_computation.1 | async-start | bytes 1572864 | tf_op jit(solution)/shard_map/all_to_all | solution.py:39
  63.5 11.0 %all-to-all-done.1 = f32[8,64,384]{2,1,0:T(8,128)S(1)} async-done(((f32[8,64,384]{2,1,0:T(8,128)}), f32[8,64,384]{2,1,0:T(8,128)S(1)}, u32[]{:S(2)}, u32[]{:S(2)}) %all-to-all-start.1) | async-done | bytes 786464 | tf_op jit(solution)/shard_map/all_to_all | solution.py:39
  74.5 0.9 divide_subtract_fusion.1
  75.4 12.3 %all_to_all.67 = f32[8,64,256]{2,1,0:T(8,128)S(1)} all-to-all(f32[8,64,256]{2,1,0:T(8,128)S(1)} %broadcast_in_dim.25), channel_id=1, replica_groups={{15,14,11,10,63,62,59,58},{12,13,8,9,60,61,56,57},{3,2,7,6,51,50,55,54}..., dimensions={0} | all-to-all | bytes 1048576 | tf_op jit(solution)/shard_map/all_to_all | solution.py:39
  88.0 0.4 broadcast_in_dim.26
  88.4 33.4 %all_to_all.68 = f32[8,8,64,256]{3,1,2,0:T(8,128)S(1)} all-to-all(f32[8,8,64,256]{3,1,2,0:T(8,128)S(1)} %broadcast_in_dim.26), channel_id=1, replica_groups={{15,12,3,0,31,28,19,16},{14,13,2,1,30,29,18,17},{11,8,7,4,27,24,23,20},..., dimensions={0} | all-to-all | bytes 8388608 | tf_op jit(solution)/shard_map/all_to_all | solution.py:39
  121.8 1.3 copy.92
  123.1 0.4 copy.112
  123.5 0.5 slice-done.2
  124.0 1.5 slice-done.3
  125.5 8.7 %fusion.9 = f32[64,256]{1,0:T(8,128)S(1)} fusion(f32[64,16384]{1,0:T(8,128)S(1)} %bitcast.70, f32[16384,256]{1,0:T(8,128)S(1)} %bitcast.64), kind=kOutput, calls=%fused_computation.35 | convolution fusion | flops 3221225472 | bytes 21037056 | tf_op jit(solution)/shard_map/dot_general | solution.py:93
  134.1 0.5 collective-permute-start
  134.6 1.2 collective-permute-done
  136.0 16.1 %fusion.10 = f32[64,16384]{1,0:T(8,128)S(1)} fusion(f32[64,256]{1,0:T(8,128)S(1)} %get-tuple-element.10, f32[16384,256]{1,0:T(8,128)S(1)} %bitcast.64), kind=kOutput, calls=%fused_computation.36 | convolution fusion | flops 3221225472 | bytes 21037056 | tf_op jit(solution)/shard_map/dot_general | solution.py:51
  152.5 0.4 pad_maximum_fusion
  152.8 35.1 %all_to_all.69 = f32[8,64,2176]{2,1,0:T(8,128)} all-to-all(f32[8,64,2176]{2,1,0:T(8,128)S(1)} %pad_maximum_fusion), channel_id=1, replica_groups={{15,12,3,0,31,28,19,16},{14,13,2,1,30,29,18,17},{11,8,7,4,27,24,23,20},..., dimensions={0} | all-to-all | bytes 8912896 | tf_op jit(solution)/shard_map/all_to_all | solution.py:39
  188.0 2.5 reduce_sum.93
  191.0 13.4 %all_to_all.70 = f32[8,64,384]{2,1,0:T(8,128)S(1)} all-to-all(f32[8,64,384]{2,1,0:T(8,128)S(1)} %copy.95), channel_id=1, replica_groups={{15,14,11,10,63,62,59,58},{12,13,8,9,60,61,56,57},{3,2,7,6,51,50,55,54}..., dimensions={0} | all-to-all | bytes 1572864 | tf_op jit(solution)/shard_map/all_to_all | solution.py:39
  204.5 0.9 divide_subtract_fusion
  205.5 12.3 %all_to_all.71 = f32[8,64,256]{2,1,0:T(8,128)S(1)} all-to-all(f32[8,64,256]{2,1,0:T(8,128)S(1)} %broadcast_in_dim.29), channel_id=1, replica_groups={{15,14,11,10,63,62,59,58},{12,13,8,9,60,61,56,57},{3,2,7,6,51,50,55,54}..., dimensions={0} | all-to-all | bytes 1048576 | tf_op jit(solution)/shard_map/all_to_all | solution.py:39
  218.1 0.4 broadcast_in_dim.30
  218.5 33.2 %all_to_all.72 = f32[8,8,64,256]{3,1,2,0:T(8,128)S(1)} all-to-all(f32[8,8,64,256]{3,1,2,0:T(8,128)S(1)} %broadcast_in_dim.30), channel_id=1, replica_groups={{15,12,3,0,31,28,19,16},{14,13,2,1,30,29,18,17},{11,8,7,4,27,24,23,20},..., dimensions={0} | all-to-all | bytes 8388608 | tf_op jit(solution)/shard_map/all_to_all | solution.py:39
  251.7 1.3 copy.98
  253.0 0.4 copy.113
  253.4 0.5 slice-done.6
  253.9 1.5 slice-done.7
  255.4 8.7 %fusion.11 = f32[64,256]{1,0:T(8,128)S(1)} fusion(f32[64,16384]{1,0:T(8,128)S(1)} %bitcast.71, f32[16384,256]{1,0:T(8,128)S(1)} %bitcast.66), kind=kOutput, calls=%fused_computation.37 | convolution fusion | flops 3221225472 | bytes 21037056 | tf_op jit(solution)/shard_map/dot_general | solution.py:93
  264.3 1.2 collective-permute-done.1
  265.8 16.2 %fusion.12 = f32[64,16384]{1,0:T(8,128)S(1)} fusion(f32[64,256]{1,0:T(8,128)S(1)} %get-tuple-element.8, f32[16384,256]{1,0:T(8,128)S(1)} %bitcast.66), kind=kOutput, calls=%fused_computation.38 | convolution fusion | flops 3221225472 | bytes 21037056 | tf_op jit(solution)/shard_map/dot_general | solution.py:51
  282.3 0.4 pad_maximum_fusion.1
  282.7 35.1 %all_to_all.73 = f32[8,64,2176]{2,1,0:T(8,128)} all-to-all(f32[8,64,2176]{2,1,0:T(8,128)S(1)} %pad_maximum_fusion.1), channel_id=1, replica_groups={{15,12,3,0,31,28,19,16},{14,13,2,1,30,29,18,17},{11,8,7,4,27,24,23,20},..., dimensions={0} | all-to-all | bytes 8912896 | tf_op jit(solution)/shard_map/all_to_all | solution.py:39
  317.8 2.5 reduce_sum.96
  320.8 13.4 %all_to_all.74 = f32[8,64,384]{2,1,0:T(8,128)S(1)} all-to-all(f32[8,64,384]{2,1,0:T(8,128)S(1)} %copy.101), channel_id=1, replica_groups={{15,14,11,10,63,62,59,58},{12,13,8,9,60,61,56,57},{3,2,7,6,51,50,55,54}..., dimensions={0} | all-to-all | bytes 1572864 | tf_op jit(solution)/shard_map/all_to_all | solution.py:39
  334.4 1.0 fusion.7
  335.4 12.0 %all_to_all.75 = f32[8,64,256]{2,1,0:T(8,128)S(1)} all-to-all(f32[8,64,256]{2,1,0:T(8,128)S(1)} %broadcast_in_dim.33), channel_id=1, replica_groups={{15,14,11,10,63,62,59,58},{12,13,8,9,60,61,56,57},{3,2,7,6,51,50,55,54}..., dimensions={0} | all-to-all | bytes 1048576 | tf_op jit(solution)/shard_map/all_to_all | solution.py:39
  347.7 0.4 broadcast_in_dim.34
  348.1 32.9 %all_to_all.76 = f32[8,8,64,256]{3,1,2,0:T(8,128)S(1)} all-to-all(f32[8,8,64,256]{3,1,2,0:T(8,128)S(1)} %broadcast_in_dim.34), channel_id=1, replica_groups={{15,12,3,0,31,28,19,16},{14,13,2,1,30,29,18,17},{11,8,7,4,27,24,23,20},..., dimensions={0} | all-to-all | bytes 8388608 | tf_op jit(solution)/shard_map/all_to_all | solution.py:39
  381.0 1.3 copy.104
  382.3 0.4 copy.114
  382.7 11.0 %fusion.13 = f32[64,256]{1,0:T(8,128)S(1)} fusion(f32[64,16384]{1,0:T(8,128)S(1)} %bitcast.72, f32[16384,256]{1,0:T(8,128)} %param.4), kind=kOutput, calls=%fused_computation.39 | convolution fusion | flops 3221225472 | bytes 21037056 | tf_op jit(solution)/shard_map/dot_general | solution.py:93
  393.8 1.2 collective-permute-done.2
  395.2 16.5 %all_to_all.77 = f32[64,1,64]{2,1,0:T(1,128)S(1)} all-to-all(f32[64,1,64]{2,1,0:T(1,128)S(1)} %broadcast_in_dim.35), channel_id=1, replica_groups=mesh['rows'=2,'z'=4,'y'=4,'x'=4] {'z','y','x'}, dimensions={0} | all-to-all | bytes 32768 | tf_op jit(solution)/shard_map/all_to_all | solution.py:105
  411.7 0.7 multiply_subtract_fusion
  (61 shorter events, 4.4 us)
Async XLA Ops:
  58.2 16.3 %all-to-all-start.1 = ((f32[8,64,384]{2,1,0:T(8,128)}), f32[8,64,384]{2,1,0:T(8,128)S(1)}, u32[]{:S(2)}, u32[]{:S(2)}) async-start(f32[8,64,384]{2,1,0:T(8,128)} %copy.90), calls=%async_computation.1 | async-start | bytes 1572864 | tf_op jit(solution)/shard_map/all_to_all | solution.py:39
  75.4 48.0 %slice-start = ((s8[16777216]{0:T(1024)(128)(4,1)}), s8[4194304]{0:T(1024)(128)(4,1)S(1)}, s32[]{:S(2)}) async-start(s8[16777216]{0:T(1024)(128)(4,1)} %bitcast.63), calls=%async_computation.13 | async-start | bytes 8388608
  88.4 35.1 %slice-start.1 = ((s8[16777216]{0:T(1024)(128)(4,1)}), s8[4194304]{0:T(1024)(128)(4,1)S(1)}, s32[]{:S(2)}) async-start(s8[16777216]{0:T(1024)(128)(4,1)} %bitcast.63), calls=%async_computation.14 | async-start | bytes 8388608
  121.8 2.2 slice-start.2
  123.1 2.4 slice-start.3
  125.5 10.4 %copy-start = (f32[64,256]{1,0:T(8,128)S(1)}, f32[64,256]{1,0:T(8,128)}, u32[]{:S(2)}) copy-start(f32[64,256]{1,0:T(8,128)} %param.6) | copy-start | bytes 196612
  125.5 10.4 %copy-start.1 = (f32[256]{0:T(256)S(1)}, f32[256]{0:T(256)}, u32[]{:S(2)}) copy-start(f32[256]{0:T(256)} %param.7) | copy-start | bytes 3076
  134.1 1.7 collective-permute-start
  205.5 47.9 %slice-start.4 = ((s8[16777216]{0:T(1024)(128)(4,1)}), s8[4194304]{0:T(1024)(128)(4,1)S(1)}, s32[]{:S(2)}) async-start(s8[16777216]{0:T(1024)(128)(4,1)} %bitcast.65), calls=%async_computation.17 | async-start | bytes 8388608
  218.5 34.9 %slice-start.5 = ((s8[16777216]{0:T(1024)(128)(4,1)}), s8[4194304]{0:T(1024)(128)(4,1)S(1)}, s32[]{:S(2)}) async-start(s8[16777216]{0:T(1024)(128)(4,1)} %bitcast.65), calls=%async_computation.18 | async-start | bytes 8388608
  251.7 2.2 slice-start.6
  253.0 2.4 slice-start.7
  264.0 1.5 collective-permute-start.1
  393.7 1.3 collective-permute-start.2

commit v2 on v1

v2 whole, which is shorter than its diff:
```python
import math

import jax
import jax.numpy as jnp
from jax import lax
from jax.experimental import pallas as pl
from jax.experimental.pallas import tpu as pltpu
from jax.sharding import Mesh
from jax.sharding import PartitionSpec as P

STEPS = 3
SIDE = 4
CUBE = 8
SHIFT = (0, 1, 1)
AXES = ("rows", "z", "y", "x")
COLS = ("z", "y", "x")
LANES = 128
TAIL = 8
F32 = jnp.float32
BF16 = jnp.bfloat16
ACROSS = (((1,), (1,)), ((), ()))
DOWN = (((1,), (0,)), ((), ()))
WHOLE = pl.BlockSpec(memory_space=pltpu.VMEM)


def place(core, at):
    turned = [(p + core + s) & (SIDE - 1) for p, s in zip(at, SHIFT)]
    half = [((t + 1) >> 1) & 1 for t in turned]
    pair = [t >> 1 for t in turned]
    return half[0] * 4 + half[1] * 2 + half[2], pair[0] * 4 + pair[1] * 2 + pair[2]


def cube_groups():
    first, second = {}, {}
    for device in range(2 * SIDE**3):
        core, z, y, x = device // 64, device // 16 % 4, device // 4 % 4, device % 4
        half, pair = place(core, (z, y, x))
        first.setdefault((core, pair), {})[half] = device
        second.setdefault((core, half), {})[pair] = device
    in_order = lambda groups: [[group[k] for k in range(CUBE)] for _, group in sorted(groups.items())]
    return in_order(first), in_order(second)


FIRST, SECOND = cube_groups()


def exchange(x, groups):
    return lax.all_to_all(x, AXES, split_axis=0, concat_axis=0, axis_index_groups=groups, tiled=True)


def own_block():
    return place(lax.axis_index("rows"), [lax.axis_index(a) for a in COLS])


def call(kernel, out_shape, name, mib, **kw):
    return pl.pallas_call(
        kernel,
        out_shape=out_shape,
        name=name,
        compiler_params=pltpu.CompilerParams(vmem_limit_bytes=mib << 20),
        **kw,
    )


def array(*shape, dtype=F32):
    return jax.ShapeDtypeStruct(shape, dtype)


def halves(x):
    high = x.astype(BF16)
    return high, (x - high.astype(F32)).astype(BF16)


def dot(a, b, dims):
    return lax.dot_general(a, b, dims, preferred_element_type=F32)


def diagonal(samples):
    shape = (samples, LANES)
    return lax.broadcasted_iota(jnp.int32, shape, 0) == lax.broadcasted_iota(jnp.int32, shape, 1)


def to_lanes(column):
    samples = column.shape[0]
    row = jnp.sum(jnp.where(diagonal(samples), column, 0.0), axis=0, keepdims=True)
    return jnp.broadcast_to(row, (TAIL, LANES))


def to_column(row, samples):
    return jnp.sum(jnp.where(diagonal(samples), row, 0.0), axis=1, keepdims=True)


def stacked(x):
    high, low = halves(x)
    return jnp.concatenate([high, low], 0), high


def put_part(out_ref, at, both, high, jac_high, jac_low, tail):
    samples = high.shape[0]
    wide = dot(both, jac_high, ACROSS)
    logits = wide[:samples] + wide[samples:] + dot(high, jac_low, ACROSS)
    tiles = logits.shape[1] // LANES
    for t in range(tiles):
        out_ref[at, t * samples : (t + 1) * samples] = logits[:, t * LANES : (t + 1) * LANES]
    out_ref[at, tiles * samples :] = tail


def open_kernel(at_ref, anchor_ref, targets_ref, jac_ref, out_ref, own_ref, high_ref, low_ref):
    part = jac_ref.shape[0]
    samples = targets_ref.shape[0]
    for t in range(targets_ref.shape[1] // LANES):
        own_ref[t * samples : (t + 1) * samples] = targets_ref[:, t * LANES : (t + 1) * LANES]
    jac_high, jac_low = halves(jac_ref[...])
    rows = pl.ds(pl.multiple_of(pl.program_id(0) * part, part), part)
    high_ref[rows] = jac_high
    low_ref[rows] = jac_low
    both, high = stacked(anchor_ref[...])
    put_part(out_ref, 0, both, high, jac_high, jac_low, jnp.zeros((TAIL, LANES), F32))


def opened(at, anchor, targets, jacobian):
    samples, cols = anchor.shape
    rows = jacobian.shape[0]
    part = rows // CUBE
    block = part // CUBE
    length = part // LANES * samples + TAIL
    return pl.pallas_call(
        open_kernel,
        name="opened",
        out_shape=[
            array(CUBE, length, LANES),
            array(block // LANES * samples, LANES),
            array(rows, cols, dtype=BF16),
            array(rows, cols, dtype=BF16),
        ],
        grid_spec=pltpu.PrefetchScalarGridSpec(
            num_scalar_prefetch=1,
            grid=(CUBE,),
            in_specs=[
                pl.BlockSpec((samples, cols), lambda i, at: (0, 0)),
                pl.BlockSpec((samples, block), lambda i, at: (0, at[0])),
                pl.BlockSpec((part, cols), lambda i, at: (i, 0)),
            ],
            out_specs=[
                pl.BlockSpec((1, length, LANES), lambda i, at: (i, 0, 0)),
                pl.BlockSpec((block // LANES * samples, LANES), lambda i, at: (0, 0)),
                WHOLE,
                WHOLE,
            ],
        ),
        compiler_params=pltpu.CompilerParams(vmem_limit_bytes=16 << 20),
    )(at, anchor, in_hbm(targets), in_hbm(jacobian))


def in_hbm(x):
    return pltpu.with_memory_space_constraint(x, pltpu.HBM)


def part_sum_kernel(in_ref, out_ref):
    length = out_ref.shape[1] - TAIL
    body = CUBE * length
    for i in range(CUBE):
        out_ref[i, :length] = jnp.sum(in_ref[:, i * length : (i + 1) * length], axis=0)
    tail = jnp.sum(in_ref[:, body:], axis=0)
    for i in range(CUBE):
        out_ref[i, length:] = tail


def part_sum(parts):
    length = (parts.shape[1] - TAIL) // CUBE + TAIL
    return call(
        part_sum_kernel, array(CUBE, length, LANES), "part_sum", 4, in_specs=[WHOLE], out_specs=WHOLE
    )(parts)


def scale_from(row, samples, clip_level, params):
    squares = to_column(row, samples)
    return jnp.minimum(1.0, clip_level / jnp.sqrt(squares / params + 1e-06))


def residual_to(out_ref, logits, targets):
    residual = jax.nn.sigmoid(logits) - targets
    for i in range(CUBE):
        out_ref[i] = residual


def first_residual_kernel(in_ref, targets_ref, residual_ref, logits_ref):
    logits = jnp.sum(in_ref[:, : targets_ref.shape[0]], axis=0)
    logits_ref[...] = logits
    residual_to(residual_ref, logits, targets_ref[...])


def first_residual(parts, targets):
    return call(
        first_residual_kernel,
        [array(CUBE, *targets.shape), array(*targets.shape)],
        "first_residual",
        4,
        in_specs=[WHOLE] * 2,
        out_specs=[WHOLE] * 2,
    )(parts, targets)


def next_residual(parts, targets, logits, slope, samples, clip_level, params):
    def kernel(in_ref, targets_ref, logits_ref, slope_ref, residual_ref, out_logits_ref, out_slope_ref, scale_ref):
        length = targets_ref.shape[0]
        row = jnp.sum(in_ref[:, length:], axis=0)[:1]
        scale = scale_from(row, samples, clip_level, params)
        scale_ref[...] = jnp.broadcast_to(scale, scale_ref.shape)
        moved = jnp.sum(in_ref[:, :length], axis=0)
        for t in range(length // samples):
            at = slice(t * samples, (t + 1) * samples)
            out_slope_ref[at] = 0.9 * slope_ref[at] + scale * moved[at]
        logits = logits_ref[...] - 0.5 * out_slope_ref[...]
        out_logits_ref[...] = logits
        residual_to(residual_ref, logits, targets_ref[...])

    shape = targets.shape
    return call(
        kernel,
        [array(CUBE, *shape), array(*shape), array(*shape), array(samples, LANES)],
        "next_residual",
        4,
        in_specs=[WHOLE] * 4,
        out_specs=[WHOLE] * 4,
    )(parts, targets, logits, slope)


def gradient_kernel(residual_ref, high_ref, low_ref, out_ref):
    samples, cols = out_ref.shape
    blocks, length, _ = residual_ref.shape
    tiles = length // samples
    rows = tiles * LANES
    wide = jnp.zeros((2 * samples, cols), F32)
    narrow = jnp.zeros((samples, cols), F32)
    for c in range(0, blocks, CUBE):
        block = [
            residual_ref[b, t * samples : (t + 1) * samples] for b in range(c, c + CUBE) for t in range(tiles)
        ]
        both, high = stacked(jnp.concatenate(block, 1))
        at = slice(c * rows, (c + CUBE) * rows)
        wide += dot(both, high_ref[at], DOWN)
        narrow += dot(high, low_ref[at], DOWN)
    out_ref[...] = wide[:samples] + wide[samples:] + narrow


def gradient_part(residual, high, low, samples):
    return call(
        gradient_kernel,
        array(samples, high.shape[1]),
        "gradient",
        16,
        in_specs=[WHOLE] * 3,
        out_specs=WHOLE,
    )(residual, high, low)


def moved_on(state):
    theta_ref, velocity_ref, gradient_ref, scale_ref = state
    velocity = 0.9 * velocity_ref[...] + scale_ref[:, :1] * gradient_ref[...]
    return theta_ref[...] - 0.5 * velocity, velocity


def whole_gradient(own_ref, other_ref, prec_ref, anchor_ref, theta):
    gradient = own_ref[...] + other_ref[...] + prec_ref[...] * (theta - anchor_ref[...])
    return gradient, jnp.sum(gradient * gradient, axis=1, keepdims=True)


def push_parts(out_ref, gradient, square, high_ref, low_ref):
    both, high = stacked(gradient)
    tail = to_lanes(square)
    part = high_ref.shape[0] // CUBE
    for j in range(CUBE):
        at = slice(j * part, (j + 1) * part)
        put_part(out_ref, j, both, high, high_ref[at], low_ref[at], tail)


def first_push_kernel(own_ref, other_ref, prec_ref, anchor_ref, high_ref, low_ref, out_ref, gradient_ref):
    gradient, square = whole_gradient(own_ref, other_ref, prec_ref, anchor_ref, anchor_ref[...])
    gradient_ref[...] = gradient
    push_parts(out_ref, gradient, square, high_ref, low_ref)


def next_push_kernel(own_ref, other_ref, prec_ref, anchor_ref, high_ref, low_ref, *refs):
    state, (out_ref, gradient_ref, theta_ref, velocity_ref) = refs[:4], refs[4:]
    theta, velocity = moved_on(state)
    theta_ref[...] = theta
    velocity_ref[...] = velocity
    gradient, square = whole_gradient(own_ref, other_ref, prec_ref, anchor_ref, theta)
    gradient_ref[...] = gradient
    push_parts(out_ref, gradient, square, high_ref, low_ref)


def pushed(own, other, prec, anchor, high, low, state=()):
    samples, cols = anchor.shape
    length = high.shape[0] // CUBE // LANES * samples + TAIL
    outs = 3 if state else 1
    return call(
        next_push_kernel if state else first_push_kernel,
        [array(CUBE, length, LANES)] + [array(samples, cols)] * outs,
        "next_push" if state else "first_push",
        16,
        in_specs=[WHOLE] * (6 + len(state)),
        out_specs=[WHOLE] * (1 + outs),
    )(own, other, prec, anchor, high, low, *state)


def last_kernel(own_ref, other_ref, prec_ref, anchor_ref, *refs):
    state, (squares_ref, gradient_ref, theta_ref, velocity_ref) = refs[:4], refs[4:]
    theta, velocity = moved_on(state)
    theta_ref[...] = theta
    velocity_ref[...] = velocity
    gradient, square = whole_gradient(own_ref, other_ref, prec_ref, anchor_ref, theta)
    gradient_ref[...] = gradient
    squares_ref[...] = jnp.broadcast_to(to_lanes(square)[:1], squares_ref.shape)


def last_gradient(own, other, prec, anchor, state):
    shape = anchor.shape
    return call(
        last_kernel,
        [array(SIDE**3, LANES)] + [array(*shape)] * 3,
        "last_gradient",
        4,
        in_specs=[WHOLE] * 8,
        out_specs=[WHOLE] * 4,
    )(own, other, prec, anchor, *state)


def close(squares, theta, velocity, gradient, clip_level, params):
    samples = theta.shape[0]

    def kernel(squares_ref, theta_ref, velocity_ref, gradient_ref, out_ref):
        row = jnp.sum(squares_ref[...], axis=0, keepdims=True)
        scale = scale_from(row, samples, clip_level, params)
        velocity = 0.9 * velocity_ref[...] + scale * gradient_ref[...]
        out_ref[...] = theta_ref[...] - 0.5 * velocity

    return call(kernel, array(*theta.shape), "close", 4, in_specs=[WHOLE] * 4, out_specs=WHOLE)(
        squares, theta, velocity, gradient
    )


def body(jacobian, targets, anchor, precision):
    samples, col_dev = anchor.shape
    row_dev = jacobian.shape[0]
    params = col_dev * SIDE**3
    clip_level = 0.2 * math.sqrt(row_dev * 2 / params)
    half, pair = own_block()
    at = jnp.reshape(half * CUBE + pair, (1,)).astype(jnp.int32)
    prec = precision[None, :]

    def summed(parts):
        return exchange(part_sum(exchange(parts, FIRST)), SECOND)

    def spread(residual):
        got = exchange(residual, SECOND)
        got = exchange(jnp.broadcast_to(got[None], (CUBE, *got.shape)), FIRST)
        return got.reshape(CUBE**2, *residual.shape[1:])

    parts, own, high, low = opened(at, anchor, targets, jacobian)
    residual, logits = first_residual(summed(parts), own)
    slope = jnp.zeros_like(logits)
    state = ()
    for step in range(STEPS):
        gradient = gradient_part(spread(residual), high, low, samples)
        other = lax.ppermute(gradient, "rows", [(0, 1), (1, 0)])
        if step + 1 == STEPS:
            break
        parts, gradient, *moved = pushed(gradient, other, prec, anchor, high, low, state)
        theta, velocity = moved if moved else (anchor, jnp.zeros_like(anchor))
        residual, logits, slope, scale = next_residual(
            summed(parts), own, logits, slope, samples, clip_level, params
        )
        state = (theta, velocity, gradient, scale)
    squares, gradient, theta, velocity = last_gradient(gradient, other, prec, anchor, state)
    squares = lax.all_to_all(squares, COLS, split_axis=0, concat_axis=0, tiled=True)
    return close(squares, theta, velocity, gradient, clip_level, params)


def solution(mesh):
    cubes = Mesh(mesh.devices.reshape(2, SIDE, SIDE, SIDE), AXES)
    in_specs = (P("rows", COLS), P(None, "rows"), P(None, COLS), P(COLS))
    out_specs = P(None, COLS)
    return jax.shard_map(body, mesh=cubes, in_specs=in_specs, out_specs=out_specs, check_vma=False)
```

time: 419 us -> 330 us (0.79); the launches traced: 413 us -> 329 us
  matrix products: 78.5 us -> 0 us
  Pallas kernels: 0 us -> 32.5 us
  other arithmetic: 12.7 us -> 0 us
  local copies, waits for them, and re-layouts: 14.6 us -> 2.37 us
  waiting for transfers between devices: 14.7 us -> 3.72 us
  starting transfers between devices: 6.17 us -> 0.44 us
  blocking collectives: 285 us -> 290 us
    dot_general x6 -> x0, matrix products: 78.5 us -> none  [the longest x3 50.2 us: product(): lax.dot_general(theta, jacobian, (((1,), (1,)), ((), ())), precision=lax....]
    pallas_call x0 -> x14, Pallas kernels: none -> 32.5 us  [the longest x1 11 us: opened(): pl.pallas_call(open_kernel, name='opened', out_shape=[array(CUBE, length,...]
    all_to_all x1 -> x0, waiting for transfers between devices: 11 us -> none  [exchange(): lax.all_to_all(x, AXES, split_axis=0, concat_axis=0, axis_index_groups=gr...]
    reduce_sum x10 -> x0, other arithmetic: 8.25 us -> none  [the longest x3 7.61 us: summed(): got = jnp.sum(exchange(jnp.concatenate([parts, tail], 2), FIRST), axis=0)]
    all_to_all x1 -> x0, starting transfers between devices: 5.31 us -> none  [exchange(): lax.all_to_all(x, AXES, split_axis=0, concat_axis=0, axis_index_groups=gr...]
    all_to_all x11 -> x12, blocking collectives: 269 us -> 274 us  [exchange(): lax.all_to_all(x, AXES, split_axis=0, concat_axis=0, axis_index_groups=gr...]
    all_to_all x6 -> x0, local copies, waits for them, and re-layouts: 4.68 us -> none  [exchange(): lax.all_to_all(x, AXES, split_axis=0, concat_axis=0, axis_index_groups=gr...]
  transfers between devices with their start and end apart: 4 -> 3, of which waited for: 4 -> 3; matrix products, arithmetic and copies ran while one was open for 0% -> 0% of each run, Pallas kernels for 0% -> 0%
where the time goes in v2:
time: 330 us; the launch traced here: 329 us
  blocking collectives  290 us (88%)
  Pallas kernels  32.5 us (10%)
  waiting for transfers between devices  3.72 us (1%)
    all_to_all x12, blocking collectives, exchange(): lax.all_to_all(x, AXES, split_axis=0, concat_axis=0, axis_index_groups=gr...  274 us
    all_to_all x1, blocking collectives, body(): lax.all_to_all(squares, COLS, split_axis=0, concat_axis=0, tiled=True)  16.5 us
    pallas_call x1, Pallas kernels, opened(): pl.pallas_call(open_kernel, name='opened', out_shape=[array(CUBE, length,...  11 us
    pallas_call x2, Pallas kernels, pushed(): call(next_push_kernel if state else first_push_kernel, [array(CUBE, lengt...  10.7 us
    pallas_call x3, Pallas kernels, gradient_part(): call(gradient_kernel, array(samples, high.shape[1]), 'gradient', 16, in_s...  8.42 us
  transfers between devices with their start and end apart: 3, of which 3 were waited for; matrix products, arithmetic and copies ran while one was open for 0% of the time, Pallas kernels for 0%

profile of v2, /device:TPU:0, one launch (start us, length us, event | category | flops | bytes accessed | tf_op | source)
XLA Modules:
  0.0 329.4 jit_solution(7336422130523636282)
XLA Ops:
  0.0 0.0 copy-start
  0.0 0.8 copy-done
  0.8 11.0 %opened.1 = (f32[8,1032,128]{2,1,0:T(8,128)S(1)}, f32[128,128]{1,0:T(8,128)S(1)}, bf16[16384,256]{1,0:T(8,128)(2,1)S(1)}, bf16[16384,256]{1,0:T(8,128)(2,1)S(1)}) custom-call(s32[1]{0:T(128)} %bitcast.at_ref, f32[64,256]{1,0:T(8,128)S(1)} %copy-done, f32[64,16384]{1,0:T(8,128)} %targets_ref.1, f32[16384,256]{1,0:T(8,128)} %jac_ref.1), custom_call_target="tpu_custom_call" | custom-call | tf_op jit(solution)/shard_map/opened/pallas_call | solution.py:127
  11.8 34.2 %all_to_all.71.in_ref = f32[8,1032,128]{2,1,0:T(8,128)S(1)} all-to-all(f32[8,1032,128]{2,1,0:T(8,128)S(1)} %get-tuple-element.27), channel_id=1, replica_groups={{15,12,3,0,31,28,19,16},{14,13,2,1,30,29,18,17},{11,8,7,4,27,24,23,20},..., dimensions={0} | all-to-all | bytes 8454144 | tf_op jit(solution)/shard_map/all_to_all | solution.py:48
  46.0 0.2 part_sum.3
  46.2 14.3 %all_to_all.72.in_ref = f32[8,136,128]{2,1,0:T(8,128)S(1)} all-to-all(f32[8,136,128]{2,1,0:T(8,128)S(1)} %part_sum.3), channel_id=1, replica_groups={{15,14,11,10,63,62,59,58},{12,13,8,9,60,61,56,57},{3,2,7,6,51,50,55,54}..., dimensions={0} | all-to-all | bytes 1114112 | tf_op jit(solution)/shard_map/all_to_all | solution.py:48
  60.5 0.1 first_residual.1
  60.6 12.0 %all_to_all.73 = f32[8,128,128]{2,1,0:T(8,128)S(1)} all-to-all(f32[8,128,128]{2,1,0:T(8,128)S(1)} %get-tuple-element.29), channel_id=1, replica_groups={{15,14,11,10,63,62,59,58},{12,13,8,9,60,61,56,57},{3,2,7,6,51,50,55,54}..., dimensions={0} | all-to-all | bytes 1048576 | tf_op jit(solution)/shard_map/all_to_all | solution.py:48
  72.6 0.5 broadcast_in_dim.12
  73.1 32.9 %all_to_all.74 = f32[8,8,128,128]{3,2,1,0:T(8,128)S(1)} all-to-all(f32[8,8,128,128]{3,2,1,0:T(8,128)S(1)} %broadcast_in_dim.12), channel_id=1, replica_groups={{15,12,3,0,31,28,19,16},{14,13,2,1,30,29,18,17},{11,8,7,4,27,24,23,20},..., dimensions={0} | all-to-all | bytes 8388608 | tf_op jit(solution)/shard_map/all_to_all | solution.py:48
  106.0 0.0 copy-start.1
  106.0 0.0 copy-start.2
  106.0 2.8 gradient.3.own_ref
  108.8 0.1 collective-permute-start
  108.9 1.2 collective-permute-done.other_ref
  110.2 0.0 copy-done.1
  110.2 0.0 copy-done.2
  110.2 5.3 %first_push.1 = (f32[8,1032,128]{2,1,0:T(8,128)S(1)}, f32[64,256]{1,0:T(8,128)S(1)}) custom-call(f32[64,256]{1,0:T(8,128)S(1)} %gradient.3.own_ref, f32[64,256]{1,0:T(8,128)S(1)} %collective-permute-done.other_ref, f32[1,256]{1,0:T(1,128)S(1)} %bitcast.14, f32[64,256]{1,0:T(8,128)S(1)} %copy-done.1, bf16[16384,256]{1,0:T(8,128)(2,1)S(1)} %get-tuple-element.30.high_ref, ...), custom_call_target="tpu_custom_call" | custom-call | tf_op jit(solution)/shard_map/first_push/pallas_call | solution.py:298
  115.5 33.1 %all_to_all.75.in_ref = f32[8,1032,128]{2,1,0:T(8,128)S(1)} all-to-all(f32[8,1032,128]{2,1,0:T(8,128)S(1)} %get-tuple-element.32), channel_id=1, replica_groups={{15,12,3,0,31,28,19,16},{14,13,2,1,30,29,18,17},{11,8,7,4,27,24,23,20},..., dimensions={0} | all-to-all | bytes 8454144 | tf_op jit(solution)/shard_map/all_to_all | solution.py:48
  148.6 0.2 part_sum.4
  148.8 12.1 %all_to_all.76.in_ref = f32[8,136,128]{2,1,0:T(8,128)S(1)} all-to-all(f32[8,136,128]{2,1,0:T(8,128)S(1)} %part_sum.4), channel_id=1, replica_groups={{15,14,11,10,63,62,59,58},{12,13,8,9,60,61,56,57},{3,2,7,6,51,50,55,54}..., dimensions={0} | all-to-all | bytes 1114112 | tf_op jit(solution)/shard_map/all_to_all | solution.py:48
  160.9 0.2 next_residual.2
  161.1 12.0 %all_to_all.77 = f32[8,128,128]{2,1,0:T(8,128)S(1)} all-to-all(f32[8,128,128]{2,1,0:T(8,128)S(1)} %get-tuple-element.34), channel_id=1, replica_groups={{15,14,11,10,63,62,59,58},{12,13,8,9,60,61,56,57},{3,2,7,6,51,50,55,54}..., dimensions={0} | all-to-all | bytes 1048576 | tf_op jit(solution)/shard_map/all_to_all | solution.py:48
  173.1 0.5 broadcast_in_dim.30
  173.6 32.9 %all_to_all.78 = f32[8,8,128,128]{3,2,1,0:T(8,128)S(1)} all-to-all(f32[8,8,128,128]{3,2,1,0:T(8,128)S(1)} %broadcast_in_dim.30), channel_id=1, replica_groups={{15,12,3,0,31,28,19,16},{14,13,2,1,30,29,18,17},{11,8,7,4,27,24,23,20},..., dimensions={0} | all-to-all | bytes 8388608 | tf_op jit(solution)/shard_map/all_to_all | solution.py:48
  206.6 2.8 gradient.4.own_ref
  209.4 0.3 collective-permute-start.1
  209.7 1.2 collective-permute-done.1.other_ref
  210.9 5.3 %next_push.1 = (f32[8,1032,128]{2,1,0:T(8,128)S(1)}, f32[64,256]{1,0:T(8,128)S(1)}, f32[64,256]{1,0:T(8,128)S(1)}, f32[64,256]{1,0:T(8,128)S(1)}) custom-call(f32[64,256]{1,0:T(8,128)S(1)} %gradient.4.own_ref, f32[64,256]{1,0:T(8,128)S(1)} %collective-permute-done.1.other_ref, f32[1,256]{1,0:T(1,128)S(1)} %bitcast.15, f32[64,256]{1,0:T(8,128)S(1)} %copy-done.1, ...), custom_call_target="tpu_custom_call" | custom-call | tf_op jit(solution)/shard_map/next_push/pallas_call | solution.py:298
  216.2 33.1 %all_to_all.79.in_ref = f32[8,1032,128]{2,1,0:T(8,128)S(1)} all-to-all(f32[8,1032,128]{2,1,0:T(8,128)S(1)} %get-tuple-element.37), channel_id=1, replica_groups={{15,12,3,0,31,28,19,16},{14,13,2,1,30,29,18,17},{11,8,7,4,27,24,23,20},..., dimensions={0} | all-to-all | bytes 8454144 | tf_op jit(solution)/shard_map/all_to_all | solution.py:48
  249.3 0.2 part_sum.5
  249.5 12.1 %all_to_all.80.in_ref = f32[8,136,128]{2,1,0:T(8,128)S(1)} all-to-all(f32[8,136,128]{2,1,0:T(8,128)S(1)} %part_sum.5), channel_id=1, replica_groups={{15,14,11,10,63,62,59,58},{12,13,8,9,60,61,56,57},{3,2,7,6,51,50,55,54}..., dimensions={0} | all-to-all | bytes 1114112 | tf_op jit(solution)/shard_map/all_to_all | solution.py:48
  261.7 0.8 next_residual.3
  262.5 12.0 %all_to_all.81 = f32[8,128,128]{2,1,0:T(8,128)S(1)} all-to-all(f32[8,128,128]{2,1,0:T(8,128)S(1)} %get-tuple-element.40), channel_id=1, replica_groups={{15,14,11,10,63,62,59,58},{12,13,8,9,60,61,56,57},{3,2,7,6,51,50,55,54}..., dimensions={0} | all-to-all | bytes 1048576 | tf_op jit(solution)/shard_map/all_to_all | solution.py:48
  274.4 0.5 broadcast_in_dim.32
  274.9 32.9 %all_to_all.82 = f32[8,8,128,128]{3,2,1,0:T(8,128)S(1)} all-to-all(f32[8,8,128,128]{3,2,1,0:T(8,128)S(1)} %broadcast_in_dim.32), channel_id=1, replica_groups={{15,12,3,0,31,28,19,16},{14,13,2,1,30,29,18,17},{11,8,7,4,27,24,23,20},..., dimensions={0} | all-to-all | bytes 8388608 | tf_op jit(solution)/shard_map/all_to_all | solution.py:48
  307.9 2.8 gradient.5.own_ref
  310.7 0.1 collective-permute-start.2
  310.8 1.2 collective-permute-done.2.other_ref
  312.0 0.2 last_gradient.1
  312.2 16.5 %all_to_all.83 = f32[64,1,128]{2,1,0:T(1,128)S(1)} all-to-all(f32[64,1,128]{2,1,0:T(1,128)S(1)} %bitcast.13), channel_id=1, replica_groups=mesh['rows'=2,'z'=4,'y'=4,'x'=4] {'z','y','x'}, dimensions={0} | all-to-all | bytes 65536 | tf_op jit(solution)/shard_map/all_to_all | solution.py:377
  328.7 0.8 close.1
  (2 shorter events, 0.0 us)
Async XLA Ops:
  0.0 0.8 copy-start
  106.0 4.2 %copy-start.1 = (f32[64,256]{1,0:T(8,128)S(1)}, f32[64,256]{1,0:T(8,128)}, u32[]{:S(2)}) copy-start(f32[64,256]{1,0:T(8,128)} %anchor_ref.7) | copy-start | bytes 196612
  106.0 4.2 %copy-start.2 = (f32[256]{0:T(256)S(1)}, f32[256]{0:T(256)}, u32[]{:S(2)}) copy-start(f32[256]{0:T(256)} %param.7) | copy-start | bytes 3076
  108.8 1.3 collective-permute-start
  209.4 1.5 collective-permute-start.1
  310.7 1.3 collective-permute-start.2

commit v3 on v2

--- a/solution.py
+++ b/solution.py
@@ -95,82 +95,76 @@
     return jnp.concatenate([high, low], 0), high
 
 
-def put_part(out_ref, at, both, high, jac_high, jac_low, tail):
+def put_parts(out_ref, both, high, jac_high_ref, jac_low_ref, tail):
     samples = high.shape[0]
-    wide = dot(both, jac_high, ACROSS)
-    logits = wide[:samples] + wide[samples:] + dot(high, jac_low, ACROSS)
-    tiles = logits.shape[1] // LANES
-    for t in range(tiles):
-        out_ref[at, t * samples : (t + 1) * samples] = logits[:, t * LANES : (t + 1) * LANES]
-    out_ref[at, tiles * samples :] = tail
-
-
-def open_kernel(at_ref, anchor_ref, targets_ref, jac_ref, out_ref, own_ref, high_ref, low_ref):
-    part = jac_ref.shape[0]
-    samples = targets_ref.shape[0]
-    for t in range(targets_ref.shape[1] // LANES):
-        own_ref[t * samples : (t + 1) * samples] = targets_ref[:, t * LANES : (t + 1) * LANES]
-    jac_high, jac_low = halves(jac_ref[...])
-    rows = pl.ds(pl.multiple_of(pl.program_id(0) * part, part), part)
-    high_ref[rows] = jac_high
-    low_ref[rows] = jac_low
-    both, high = stacked(anchor_ref[...])
-    put_part(out_ref, 0, both, high, jac_high, jac_low, jnp.zeros((TAIL, LANES), F32))
-
-
-def opened(at, anchor, targets, jacobian):
-    samples, cols = anchor.shape
-    rows = jacobian.shape[0]
+    rows = jac_high_ref.shape[0]
     part = rows // CUBE
-    block = part // CUBE
-    length = part // LANES * samples + TAIL
+    tiles = part // LANES
+    for j in range(CUBE):
+        at = slice(j * part, (j + 1) * part)
+        wide = dot(both, jac_high_ref[at], ACROSS)
+        logits = wide[:samples] + wide[samples:] + dot(high, jac_low_ref[at], ACROSS)
+        for t in range(tiles):
+            out_ref[j, t * samples : (t + 1) * samples] = logits[:, t * LANES : (t + 1) * LANES]
+        out_ref[j, tiles * samples :] = tail
+
+
+def open_kernel(at_ref, theta_ref, targets_ref, jac_ref, out_ref, own_ref, high_ref, low_ref, both_ref):
+    samples, cols = theta_ref.shape[1:]
+    member = pl.program_id(0)
+    lanes = pl.ds(pl.multiple_of(member * cols, cols), cols)
+    jac_high, jac_low = halves(jac_ref[0])
+    high_ref[:, lanes] = jac_high
+    low_ref[:, lanes] = jac_low
+    both_ref[:, lanes], _ = stacked(theta_ref[0])
+
+    @pl.when(member == CUBE - 1)
+    def _():
+        for t in range(targets_ref.shape[1] // LANES):
+            own_ref[t * samples : (t + 1) * samples] = targets_ref[:, t * LANES : (t + 1) * LANES]
+        both = both_ref[...]
+        put_parts(out_ref, both, both[:samples], high_ref, low_ref, jnp.zeros((TAIL, LANES), F32))
+
+
+def opened(at, theta, targets, jacobian):
+    samples, cols = theta.shape[1:]
+    rows = jacobian.shape[1]
+    block = rows // CUBE
+    length = block // LANES * samples
     return pl.pallas_call(
         open_kernel,
         name="opened",
         out_shape=[
-            array(CUBE, length, LANES),
-            array(block // LANES * samples, LANES),
-            array(rows, cols, dtype=BF16),
-            array(rows, cols, dtype=BF16),
+            array(CUBE, length + TAIL, LANES),
+            array(length, LANES),
+            array(rows, CUBE * cols, dtype=BF16),
+            array(rows, CUBE * cols, dtype=BF16),
         ],
         grid_spec=pltpu.PrefetchScalarGridSpec(
             num_scalar_prefetch=1,
             grid=(CUBE,),
             in_specs=[
-                pl.BlockSpec((samples, cols), lambda i, at: (0, 0)),
+                pl.BlockSpec((1, samples, cols), lambda i, at: (i, 0, 0)),
                 pl.BlockSpec((samples, block), lambda i, at: (0, at[0])),
-                pl.BlockSpec((part, cols), lambda i, at: (i, 0)),
+                pl.BlockSpec((1, rows, cols), lambda i, at: (i, 0, 0)),
             ],
-            out_specs=[
-                pl.BlockSpec((1, length, LANES), lambda i, at: (i, 0, 0)),
-                pl.BlockSpec((block // LANES * samples, LANES), lambda i, at: (0, 0)),
-                WHOLE,
-                WHOLE,
-            ],
+            out_specs=[WHOLE] * 4,
+            scratch_shapes=[pltpu.VMEM((2 * samples, CUBE * cols), BF16)],
         ),
         compiler_params=pltpu.CompilerParams(vmem_limit_bytes=16 << 20),
-    )(at, anchor, in_hbm(targets), in_hbm(jacobian))
+    )(at, theta, in_hbm(targets), in_hbm(jacobian))
 
 
 def in_hbm(x):
     return pltpu.with_memory_space_constraint(x, pltpu.HBM)
 
 
-def part_sum_kernel(in_ref, out_ref):
-    length = out_ref.shape[1] - TAIL
-    body = CUBE * length
-    for i in range(CUBE):
-        out_ref[i, :length] = jnp.sum(in_ref[:, i * length : (i + 1) * length], axis=0)
-    tail = jnp.sum(in_ref[:, body:], axis=0)
-    for i in range(CUBE):
-        out_ref[i, length:] = tail
-
-
-def part_sum(parts):
-    length = (parts.shape[1] - TAIL) // CUBE + TAIL
-    return call(
-        part_sum_kernel, array(CUBE, length, LANES), "part_sum", 4, in_specs=[WHOLE], out_specs=WHOLE
-    )(parts)
+def fold_kernel(in_ref, out_ref):
+    out_ref[...] = jnp.sum(in_ref[...], axis=0)
+
+
+def fold(parts):
+    return call(fold_kernel, array(*parts.shape[1:]), "fold", 4, in_specs=[WHOLE], out_specs=WHOLE)(parts)
 
 
 def scale_from(row, samples, clip_level, params):
@@ -226,28 +220,24 @@
     )(parts, targets, logits, slope)
 
 
+def joined(in_ref, samples):
+    blocks, length = in_ref.shape[0], in_ref.shape[1] // samples * samples
+    return jnp.concatenate([in_ref[b, t : t + samples] for b in range(blocks) for t in range(0, length, samples)], 1)
+
+
 def gradient_kernel(residual_ref, high_ref, low_ref, out_ref):
-    samples, cols = out_ref.shape
-    blocks, length, _ = residual_ref.shape
-    tiles = length // samples
-    rows = tiles * LANES
-    wide = jnp.zeros((2 * samples, cols), F32)
-    narrow = jnp.zeros((samples, cols), F32)
-    for c in range(0, blocks, CUBE):
-        block = [
-            residual_ref[b, t * samples : (t + 1) * samples] for b in range(c, c + CUBE) for t in range(tiles)
-        ]
-        both, high = stacked(jnp.concatenate(block, 1))
-        at = slice(c * rows, (c + CUBE) * rows)
-        wide += dot(both, high_ref[at], DOWN)
-        narrow += dot(high, low_ref[at], DOWN)
-    out_ref[...] = wide[:samples] + wide[samples:] + narrow
-
-
-def gradient_part(residual, high, low, samples):
+    samples, cols = out_ref.shape[1:]
+    both, high = stacked(joined(residual_ref, samples))
+    for c in range(CUBE):
+        at = slice(c * cols, (c + 1) * cols)
+        wide = dot(both, high_ref[:, at], DOWN)
+        out_ref[c] = wide[:samples] + wide[samples:] + dot(high, low_ref[:, at], DOWN)
+
+
+def gradient_parts(residual, high, low, samples):
     return call(
         gradient_kernel,
-        array(samples, high.shape[1]),
+        array(CUBE, samples, high.shape[1] // CUBE),
         "gradient",
         16,
         in_specs=[WHOLE] * 3,
@@ -266,43 +256,59 @@
     return gradient, jnp.sum(gradient * gradient, axis=1, keepdims=True)
 
 
-def push_parts(out_ref, gradient, square, high_ref, low_ref):
-    both, high = stacked(gradient)
+def send_gradient(out_ref, gradient, square):
+    samples, cols = gradient.shape
     tail = to_lanes(square)
-    part = high_ref.shape[0] // CUBE
-    for j in range(CUBE):
-        at = slice(j * part, (j + 1) * part)
-        put_part(out_ref, j, both, high, high_ref[at], low_ref[at], tail)
-
-
-def first_push_kernel(own_ref, other_ref, prec_ref, anchor_ref, high_ref, low_ref, out_ref, gradient_ref):
+    for c in range(CUBE):
+        for t in range(cols // LANES):
+            out_ref[c, t * samples : (t + 1) * samples] = gradient[:, t * LANES : (t + 1) * LANES]
+        out_ref[c, cols // LANES * samples :] = tail
+
+
+def first_step_kernel(own_ref, other_ref, prec_ref, anchor_ref, out_ref, gradient_ref):
     gradient, square = whole_gradient(own_ref, other_ref, prec_ref, anchor_ref, anchor_ref[...])
     gradient_ref[...] = gradient
-    push_parts(out_ref, gradient, square, high_ref, low_ref)
-
-
-def next_push_kernel(own_ref, other_ref, prec_ref, anchor_ref, high_ref, low_ref, *refs):
+    send_gradient(out_ref, gradient, square)
+
+
+def next_step_kernel(own_ref, other_ref, prec_ref, anchor_ref, *refs):
     state, (out_ref, gradient_ref, theta_ref, velocity_ref) = refs[:4], refs[4:]
     theta, velocity = moved_on(state)
     theta_ref[...] = theta
     velocity_ref[...] = velocity
     gradient, square = whole_gradient(own_ref, other_ref, prec_ref, anchor_ref, theta)
     gradient_ref[...] = gradient
-    push_parts(out_ref, gradient, square, high_ref, low_ref)
-
-
-def pushed(own, other, prec, anchor, high, low, state=()):
+    send_gradient(out_ref, gradient, square)
+
+
+def stepped(own, other, prec, anchor, state=()):
     samples, cols = anchor.shape
-    length = high.shape[0] // CUBE // LANES * samples + TAIL
     outs = 3 if state else 1
     return call(
-        next_push_kernel if state else first_push_kernel,
-        [array(CUBE, length, LANES)] + [array(samples, cols)] * outs,
-        "next_push" if state else "first_push",
+        next_step_kernel if state else first_step_kernel,
+        [array(CUBE, cols // LANES * samples + TAIL, LANES)] + [array(samples, cols)] * outs,
+        "next_step" if state else "first_step",
+        4,
+        in_specs=[WHOLE] * (4 + len(state)),
+        out_specs=[WHOLE] * (1 + outs),
+    )(own, other, prec, anchor, *state)
+
+
+def push(parts, high, low, samples):
+    def kernel(in_ref, high_ref, low_ref, out_ref):
+        both, first = stacked(joined(in_ref, samples))
+        tail = jnp.sum(in_ref[:, -TAIL:], axis=0)
+        put_parts(out_ref, both, first, high_ref, low_ref, tail)
+
+    rows = high.shape[0]
+    return call(
+        kernel,
+        array(CUBE, rows // CUBE // LANES * samples + TAIL, LANES),
+        "push",
         16,
-        in_specs=[WHOLE] * (6 + len(state)),
-        out_specs=[WHOLE] * (1 + outs),
-    )(own, other, prec, anchor, high, low, *state)
+        in_specs=[WHOLE] * 3,
+        out_specs=WHOLE,
+    )(parts, high, low)
 
 
 def last_kernel(own_ref, other_ref, prec_ref, anchor_ref, *refs):
@@ -347,31 +353,24 @@
     params = col_dev * SIDE**3
     clip_level = 0.2 * math.sqrt(row_dev * 2 / params)
     half, pair = own_block()
-    at = jnp.reshape(half * CUBE + pair, (1,)).astype(jnp.int32)
+    at = jnp.reshape(pair * CUBE + half, (1,)).astype(jnp.int32)
     prec = precision[None, :]
-
-    def summed(parts):
-        return exchange(part_sum(exchange(parts, FIRST)), SECOND)
-
-    def spread(residual):
-        got = exchange(residual, SECOND)
-        got = exchange(jnp.broadcast_to(got[None], (CUBE, *got.shape)), FIRST)
-        return got.reshape(CUBE**2, *residual.shape[1:])
-
-    parts, own, high, low = opened(at, anchor, targets, jacobian)
-    residual, logits = first_residual(summed(parts), own)
+    theta = exchange(jnp.broadcast_to(anchor[None], (CUBE, samples, col_dev)), SECOND)
+    square = exchange(jacobian.reshape(CUBE, row_dev // CUBE, col_dev), SECOND)
+    parts, own, high, low = opened(at, theta, targets, square)
+    residual, logits = first_residual(exchange(parts, FIRST), own)
     slope = jnp.zeros_like(logits)
     state = ()
     for step in range(STEPS):
-        gradient = gradient_part(spread(residual), high, low, samples)
+        parts = gradient_parts(exchange(residual, FIRST), high, low, samples)
+        gradient = fold(exchange(parts, SECOND))
         other = lax.ppermute(gradient, "rows", [(0, 1), (1, 0)])
         if step + 1 == STEPS:
             break
-        parts, gradient, *moved = pushed(gradient, other, prec, anchor, high, low, state)
+        parts, gradient, *moved = stepped(gradient, other, prec, anchor, state)
         theta, velocity = moved if moved else (anchor, jnp.zeros_like(anchor))
-        residual, logits, slope, scale = next_residual(
-            summed(parts), own, logits, slope, samples, clip_level, params
-        )
+        parts = exchange(push(exchange(parts, SECOND), high, low, samples), FIRST)
+        residual, logits, slope, scale = next_residual(parts, own, logits, slope, samples, clip_level, params)
         state = (theta, velocity, gradient, scale)
     squares, gradient, theta, velocity = last_gradient(gradient, other, prec, anchor, state)
     squares = lax.all_to_all(squares, COLS, split_axis=0, concat_axis=0, tiled=True)

time: 330 us -> 332 us (level)
  blocking collectives: 290 us -> 178 us
  waiting for transfers between devices: 3.72 us -> 111 us
  starting transfers between devices: 0.44 us -> 5.99 us
    all_to_all x12, blocking collectives: 274 us -> 162 us  [exchange(): lax.all_to_all(x, AXES, split_axis=0, concat_axis=0, axis_index_groups=gr...]
    all_to_all x0 -> x1, waiting for transfers between devices: none -> 107 us  [exchange(): lax.all_to_all(x, AXES, split_axis=0, concat_axis=0, axis_index_groups=gr...]
    all_to_all x0 -> x1, starting transfers between devices: none -> 5.73 us  [exchange(): lax.all_to_all(x, AXES, split_axis=0, concat_axis=0, axis_index_groups=gr...]
    pallas_call x9 -> x11, Pallas kernels: 30.6 us -> 33.7 us  [the longest x1 14.4 us: opened(): pl.pallas_call(open_kernel, name='opened', out_shape=[array(CUBE, length...]
  transfers between devices with their start and end apart: 3 -> 4, of which waited for: 3 -> 4; matrix products, arithmetic and copies ran while one was open for 0% -> 0% of each run, Pallas kernels for 0% -> 0%
where the time goes in v3:
time: 332 us; the launch traced here: 331 us
  blocking collectives  178 us (54%)
  waiting for transfers between devices  111 us (33%)
  Pallas kernels  35.6 us (11%)
  starting transfers between devices  5.99 us (2%)
    all_to_all x12, blocking collectives, exchange(): lax.all_to_all(x, AXES, split_axis=0, concat_axis=0, axis_index_groups=gr...  162 us
    all_to_all x1, waiting for transfers between devices, exchange(): lax.all_to_all(x, AXES, split_axis=0, concat_axis=0, axis_index_groups=gr...  107 us
    all_to_all x1, blocking collectives, body(): lax.all_to_all(squares, COLS, split_axis=0, concat_axis=0, tiled=True)  16.5 us
    pallas_call x1, Pallas kernels, opened(): pl.pallas_call(open_kernel, name='opened', out_shape=[array(CUBE, length...  14.4 us
    pallas_call x2, Pallas kernels, push(): call(kernel, array(CUBE, rows // CUBE // LANES * samples + TAIL, LANES),...  10.7 us
    pallas_call x3, Pallas kernels, gradient_parts(): call(gradient_kernel, array(CUBE, samples, high.shape[1] // CUBE), 'gradi...  8.25 us
  transfers between devices with their start and end apart: 4, of which 4 were waited for; matrix products, arithmetic and copies ran while one was open for 0% of the time, Pallas kernels for 0%

profile of v3, /device:TPU:0, one launch (start us, length us, event | category | flops | bytes accessed | tf_op | source)
XLA Modules:
  0.0 331.5 jit_solution(14774988806675791204)
XLA Ops:
  0.0 0.9 broadcast_in_dim.15
  0.9 16.7 %all_to_all.76.theta_ref = f32[8,64,256]{2,1,0:T(8,128)S(1)} all-to-all(f32[8,64,256]{2,1,0:T(8,128)S(1)} %broadcast_in_dim.15), channel_id=1, replica_groups={{15,14,11,10,63,62,59,58},{12,13,8,9,60,61,56,57},{3,2,7,6,51,50,55,54}..., dimensions={0} | all-to-all | bytes 1048576 | tf_op jit(solution)/shard_map/all_to_all | solution.py:48
  17.6 5.7 %all-to-all-start.1 = ((f32[8,2048,256]{2,1,0:T(8,128)}), f32[8,2048,256]{2,1,0:T(8,128)}, u32[]{:S(2)}, u32[]{:S(2)}) async-start(f32[8,2048,256]{2,1,0:T(8,128)} %bitcast.12), calls=%async_computation.1 | async-start | bytes 33554432 | tf_op jit(solution)/shard_map/all_to_all | solution.py:48
  23.4 106.9 %all-to-all-done.1.jac_ref = f32[8,2048,256]{2,1,0:T(8,128)} async-done(((f32[8,2048,256]{2,1,0:T(8,128)}), f32[8,2048,256]{2,1,0:T(8,128)}, u32[]{:S(2)}, u32[]{:S(2)}) %all-to-all-start.1) | async-done | bytes 16777248 | tf_op jit(solution)/shard_map/all_to_all | solution.py:48
  130.3 14.4 %opened.1 = (f32[8,136,128]{2,1,0:T(8,128)S(1)}, f32[128,128]{1,0:T(8,128)S(1)}, bf16[2048,2048]{1,0:T(8,128)(2,1)S(1)}, bf16[2048,2048]{1,0:T(8,128)(2,1)S(1)}) custom-call(s32[1]{0:T(128)} %bitcast.at_ref, f32[8,64,256]{2,1,0:T(8,128)S(1)} %all_to_all.76.theta_ref, f32[64,16384]{1,0:T(8,128)} %targets_ref.1, f32[8,2048,256]{2,1,0:T(8,128)} %all-to-all-done.1.jac_ref), custom_call_target="tpu_custom_call" | custom-call | tf_op jit(solution)/shard_map/opened/pallas_call | solution.py:134
  144.7 12.6 %all_to_all.77.in_ref = f32[8,136,128]{2,1,0:T(8,128)S(1)} all-to-all(f32[8,136,128]{2,1,0:T(8,128)S(1)} %get-tuple-element.27), channel_id=1, replica_groups={{15,12,3,0,31,28,19,16},{14,13,2,1,30,29,18,17},{11,8,7,4,27,24,23,20},..., dimensions={0} | all-to-all | bytes 1114112 | tf_op jit(solution)/shard_map/all_to_all | solution.py:48
  157.3 0.1 first_residual.1
  157.4 13.2 %all_to_all.78.residual_ref = f32[8,128,128]{2,1,0:T(8,128)S(1)} all-to-all(f32[8,128,128]{2,1,0:T(8,128)S(1)} %get-tuple-element.29), channel_id=1, replica_groups={{15,12,3,0,31,28,19,16},{14,13,2,1,30,29,18,17},{11,8,7,4,27,24,23,20},..., dimensions={0} | all-to-all | bytes 1048576 | tf_op jit(solution)/shard_map/all_to_all | solution.py:48
  170.6 0.0 copy-start
  170.6 0.0 copy-start.1
  170.6 2.7 gradient.3
  173.3 18.5 %all_to_all.79.in_ref = f32[8,64,256]{2,1,0:T(8,128)S(1)} all-to-all(f32[8,64,256]{2,1,0:T(8,128)S(1)} %gradient.3), channel_id=1, replica_groups={{15,14,11,10,63,62,59,58},{12,13,8,9,60,61,56,57},{3,2,7,6,51,50,55,54}..., dimensions={0} | all-to-all | bytes 1048576 | tf_op jit(solution)/shard_map/all_to_all | solution.py:48
  191.9 0.1 collective-permute-start
  191.9 1.2 collective-permute-done.other_ref
  193.2 0.0 copy-done
  193.2 0.0 copy-done.1
  193.2 0.1 first_step.1
  193.3 12.1 %all_to_all.80.in_ref = f32[8,136,128]{2,1,0:T(8,128)S(1)} all-to-all(f32[8,136,128]{2,1,0:T(8,128)S(1)} %get-tuple-element.32), channel_id=1, replica_groups={{15,14,11,10,63,62,59,58},{12,13,8,9,60,61,56,57},{3,2,7,6,51,50,55,54}..., dimensions={0} | all-to-all | bytes 1114112 | tf_op jit(solution)/shard_map/all_to_all | solution.py:48
  205.5 5.3 %push.2 = f32[8,136,128]{2,1,0:T(8,128)S(1)} custom-call(f32[8,136,128]{2,1,0:T(8,128)S(1)} %all_to_all.80.in_ref, bf16[2048,2048]{1,0:T(8,128)(2,1)S(1)} %get-tuple-element.30.high_ref, bf16[2048,2048]{1,0:T(8,128)(2,1)S(1)} %get-tuple-element.31.low_ref), custom_call_target="tpu_custom_call" | custom-call | tf_op jit(solution)/shard_map/push/pallas_call | solution.py:304
  210.8 12.6 %all_to_all.81.in_ref = f32[8,136,128]{2,1,0:T(8,128)S(1)} all-to-all(f32[8,136,128]{2,1,0:T(8,128)S(1)} %push.2), channel_id=1, replica_groups={{15,12,3,0,31,28,19,16},{14,13,2,1,30,29,18,17},{11,8,7,4,27,24,23,20},..., dimensions={0} | all-to-all | bytes 1114112 | tf_op jit(solution)/shard_map/all_to_all | solution.py:48
  223.4 0.2 next_residual.2
  223.6 13.2 %all_to_all.82.residual_ref = f32[8,128,128]{2,1,0:T(8,128)S(1)} all-to-all(f32[8,128,128]{2,1,0:T(8,128)S(1)} %get-tuple-element.34), channel_id=1, replica_groups={{15,12,3,0,31,28,19,16},{14,13,2,1,30,29,18,17},{11,8,7,4,27,24,23,20},..., dimensions={0} | all-to-all | bytes 1048576 | tf_op jit(solution)/shard_map/all_to_all | solution.py:48
  236.8 2.8 gradient.4
  239.6 12.0 %all_to_all.83.in_ref = f32[8,64,256]{2,1,0:T(8,128)S(1)} all-to-all(f32[8,64,256]{2,1,0:T(8,128)S(1)} %gradient.4), channel_id=1, replica_groups={{15,14,11,10,63,62,59,58},{12,13,8,9,60,61,56,57},{3,2,7,6,51,50,55,54}..., dimensions={0} | all-to-all | bytes 1048576 | tf_op jit(solution)/shard_map/all_to_all | solution.py:48
  251.6 0.1 collective-permute-start.1
  251.7 1.2 collective-permute-done.1.other_ref
  252.9 0.2 next_step.1
  253.1 12.1 %all_to_all.84.in_ref = f32[8,136,128]{2,1,0:T(8,128)S(1)} all-to-all(f32[8,136,128]{2,1,0:T(8,128)S(1)} %get-tuple-element.37), channel_id=1, replica_groups={{15,14,11,10,63,62,59,58},{12,13,8,9,60,61,56,57},{3,2,7,6,51,50,55,54}..., dimensions={0} | all-to-all | bytes 1114112 | tf_op jit(solution)/shard_map/all_to_all | solution.py:48
  265.3 5.3 %push.3 = f32[8,136,128]{2,1,0:T(8,128)S(1)} custom-call(f32[8,136,128]{2,1,0:T(8,128)S(1)} %all_to_all.84.in_ref, bf16[2048,2048]{1,0:T(8,128)(2,1)S(1)} %get-tuple-element.30.high_ref, bf16[2048,2048]{1,0:T(8,128)(2,1)S(1)} %get-tuple-element.31.low_ref), custom_call_target="tpu_custom_call" | custom-call | tf_op jit(solution)/shard_map/push/pallas_call | solution.py:304
  270.6 13.4 %all_to_all.85.in_ref = f32[8,136,128]{2,1,0:T(8,128)S(1)} all-to-all(f32[8,136,128]{2,1,0:T(8,128)S(1)} %push.3), channel_id=1, replica_groups={{15,12,3,0,31,28,19,16},{14,13,2,1,30,29,18,17},{11,8,7,4,27,24,23,20},..., dimensions={0} | all-to-all | bytes 1114112 | tf_op jit(solution)/shard_map/all_to_all | solution.py:48
  284.0 0.8 next_residual.3
  284.8 13.2 %all_to_all.86.residual_ref = f32[8,128,128]{2,1,0:T(8,128)S(1)} all-to-all(f32[8,128,128]{2,1,0:T(8,128)S(1)} %get-tuple-element.40), channel_id=1, replica_groups={{15,12,3,0,31,28,19,16},{14,13,2,1,30,29,18,17},{11,8,7,4,27,24,23,20},..., dimensions={0} | all-to-all | bytes 1048576 | tf_op jit(solution)/shard_map/all_to_all | solution.py:48
  298.0 2.7 gradient.5
  300.7 12.0 %all_to_all.87.in_ref = f32[8,64,256]{2,1,0:T(8,128)S(1)} all-to-all(f32[8,64,256]{2,1,0:T(8,128)S(1)} %gradient.5), channel_id=1, replica_groups={{15,14,11,10,63,62,59,58},{12,13,8,9,60,61,56,57},{3,2,7,6,51,50,55,54}..., dimensions={0} | all-to-all | bytes 1048576 | tf_op jit(solution)/shard_map/all_to_all | solution.py:48
  312.7 0.1 collective-permute-start.2
  312.8 1.2 collective-permute-done.2.other_ref
  314.1 0.2 last_gradient.1
  314.3 16.5 %all_to_all.88 = f32[64,1,128]{2,1,0:T(1,128)S(1)} all-to-all(f32[64,1,128]{2,1,0:T(1,128)S(1)} %bitcast.8), channel_id=1, replica_groups=mesh['rows'=2,'z'=4,'y'=4,'x'=4] {'z','y','x'}, dimensions={0} | all-to-all | bytes 65536 | tf_op jit(solution)/shard_map/all_to_all | solution.py:376
  330.7 0.8 close.1
  (5 shorter events, 0.1 us)
Async XLA Ops:
  17.6 112.7 %all-to-all-start.1 = ((f32[8,2048,256]{2,1,0:T(8,128)}), f32[8,2048,256]{2,1,0:T(8,128)}, u32[]{:S(2)}, u32[]{:S(2)}) async-start(f32[8,2048,256]{2,1,0:T(8,128)} %bitcast.12), calls=%async_computation.1 | async-start | bytes 33554432 | tf_op jit(solution)/shard_map/all_to_all | solution.py:48
  170.6 22.6 %copy-start = (f32[64,256]{1,0:T(8,128)S(1)}, f32[64,256]{1,0:T(8,128)}, u32[]{:S(2)}) copy-start(f32[64,256]{1,0:T(8,128)} %anchor_ref.5) | copy-start | bytes 196612
  170.6 22.6 %copy-start.1 = (f32[256]{0:T(256)S(1)}, f32[256]{0:T(256)}, u32[]{:S(2)}) copy-start(f32[256]{0:T(256)} %param.7) | copy-start | bytes 3076
  191.9 1.3 collective-permute-start
  251.6 1.3 collective-permute-start.1
  312.7 1.3 collective-permute-start.2
